TPU v7x, 32 devices: a whole 2x2x4 slice. The times are simulated.
32 devices in a mesh: gr: 4 (over z), gc: 8 (over y, x, core).
Axes of the slice: x: 2, y: 2, z: 4, core: 2. Of those that a mesh axis runs over, the one named last changes fastest.
Arguments:
- student: bfloat16 [4096, 1024], P(('gr', 'gc')), may hold values from -500 to 500
- teacher: bfloat16 [4096, 1024], P(('gr', 'gc')), may hold values from -500 to 500
Outputs:
- student_grad: float32 [4096, 1024], P(('gr', 'gc'))
All inputs are finite; a program needn't handle non-finite values.
Results may differ from a plain program's by a relative error of at most 0.0085.
Values may be sent and summed in bfloat16 or wider, within the bound.
No kernel may reach another device: no remote copies, remote signals or barrier semaphores. Data moves between devices by JAX's collectives and lax.ppermute only.
A program may use at most 64 MiB of HBM per device.

v0:
```python
import jax
import jax.numpy as jnp
from jax import lax
from jax.sharding import PartitionSpec as P

D = 1024


def unit_rows(embedded):
    values = embedded.astype(jnp.float32)
    inverse_rms = lax.rsqrt(jnp.mean(values * values, axis=-1, keepdims=True) + 1e-06)
    unit = (values * inverse_rms * D ** (-0.5)).astype(jnp.bfloat16)
    return (unit, inverse_rms)


def mismatch_of(piece_s, piece_t, other_s, other_t):
    sim_student = lax.dot_general(
        piece_s, other_s, (((1,), (1,)), ((), ())), preferred_element_type=jnp.float32
    )
    sim_teacher = lax.dot_general(
        piece_t, other_t, (((1,), (1,)), ((), ())), preferred_element_type=jnp.float32
    )
    stretch = 0.5 * D**0.5
    return jnp.tanh(stretch * (sim_student - sim_teacher)).astype(jnp.bfloat16)


def local(student, teacher):
    unit_s, inv_s = unit_rows(student)
    unit_t, inv_t = unit_rows(teacher)
    column_s, column_t = (
        lax.all_gather(unit_s, "gr", axis=0, tiled=True),
        lax.all_gather(unit_t, "gr", axis=0, tiled=True),
    )
    piece_s = lax.all_gather(unit_s, "gc", axis=0, tiled=True)
    piece_t = lax.all_gather(unit_t, "gc", axis=0, tiled=True)
    mismatch = mismatch_of(piece_s, piece_t, column_s, column_t)
    carried = lax.dot_general(
        mismatch, piece_s, (((0,), (0,)), ((), ())), preferred_element_type=jnp.float32
    )
    pull = lax.psum_scatter(carried, "gr", scatter_dimension=0, tiled=True)
    unit_float = unit_s.astype(jnp.float32)
    radial = jnp.sum(unit_float * pull, axis=-1, keepdims=True)
    total_rows = unit_s.shape[0] * lax.axis_size("gr") * lax.axis_size("gc")
    factor = 12.0 * (D / total_rows) ** 0.5
    return factor * inv_s * (pull - radial * unit_float)


def solution(mesh):
    in_specs = (P(("gr", "gc"), None), P(("gr", "gc"), None))
    out_specs = P(("gr", "gc"), None)
    return jax.shard_map(local, mesh=mesh, in_specs=in_specs, out_specs=out_specs, check_vma=False)
```

profile of v0, /device:TPU:0, one launch (start us, length us, event | category | flops | bytes accessed | tf_op | source)
XLA Modules:
  0.0 187.9 jit_solution(5423686631979588535)
XLA Ops:
  6.5 0.0 all-gather.7.cloned.1.call-start
  6.5 1.1 fusion.1
  7.6 1.8 fusion.3
  9.4 0.0 all-gather.7.cloned.1.call-update
  9.4 0.0 all-gather.5.cloned.1.call-start
  9.5 0.7 all-gather.5.cloned.1.call-update
  10.2 0.0 all-gather.11.cloned.1.call-start
  10.2 1.1 fusion.4
  11.3 1.8 fusion.6
  13.1 0.0 all-gather.11.cloned.1.call-update
  13.2 0.0 all-gather.9.cloned.1.call-start
  13.2 0.5 all-gather.9.cloned.1.call-update
  13.8 0.0 reduce-scatter.2.cloned.1.call-start
  13.8 26.5 %all-gather.7.cloned.1.call-done = bf16[512,1024]{1,0:T(8,128)(2,1)} async-done(((bf16[128,1024]{1,0:T(8,128)(2,1)}), bf16[512,1024]{1,0:T(8,128)(2,1)}) %all-gather.7.cloned.1.call-update) | async-done | bytes 1048592 | tf_op jit(solution)/shard_map/all_gather | solution.py:31
  40.3 29.1 %all-gather.5.cloned.1.call-done = bf16[1024,1024]{1,0:T(8,128)(2,1)} async-done(((bf16[128,1024]{1,0:T(8,128)(2,1)}), bf16[1024,1024]{1,0:T(8,128)(2,1)}) %all-gather.5.cloned.1.call-update) | async-done | bytes 2097168 | tf_op jit(solution)/shard_map/all_gather | solution.py:34
  69.4 4.6 %fusion.11 = f32[1024,512]{1,0:T(8,128)} fusion(bf16[1024,1024]{1,0:T(8,128)(2,1)} %all-gather.5.cloned.1.call-done, bf16[512,1024]{1,0:T(8,128)(2,1)} %all-gather.7.cloned.1.call-done), kind=kOutput, calls=%fused_computation.21 | convolution fusion | flops 1073741824 | bytes 5242880 | tf_op jit(solution)/shard_map/dot_general | solution.py:17
  74.0 25.0 %all-gather.11.cloned.1.call-done = bf16[512,1024]{1,0:T(8,128)(2,1)} async-done(((bf16[128,1024]{1,0:T(8,128)(2,1)}), bf16[512,1024]{1,0:T(8,128)(2,1)}) %all-gather.11.cloned.1.call-update) | async-done | bytes 1048592 | tf_op jit(solution)/shard_map/all_gather | solution.py:32
  99.0 28.9 %all-gather.9.cloned.1.call-done = bf16[1024,1024]{1,0:T(8,128)(2,1)} async-done(((bf16[128,1024]{1,0:T(8,128)(2,1)}), bf16[1024,1024]{1,0:T(8,128)(2,1)}) %all-gather.9.cloned.1.call-update) | async-done | bytes 2097168 | tf_op jit(solution)/shard_map/all_gather | solution.py:35
  127.9 6.4 %fusion = f32[512,1024]{1,0:T(8,128)} fusion(bf16[1024,1024]{1,0:T(8,128)(2,1)S(1)} %copy-done.1, f32[1024,512]{1,0:T(8,128)} %fusion.11, bf16[1024,1024]{1,0:T(8,128)(2,1)} %all-gather.9.cloned.1.call-done, bf16[512,1024]{1,0:T(8,128)(2,1)} %all-gather.11.cloned.1.call-done), kind=kOutput, calls=%fused_computation.1 | convolution fusion | flops 2149056512 | bytes 9437184 | tf_op jit(solution)/shard_map/dot_general | solution.py:37
  134.3 0.0 reduce-scatter.2.cloned.1.call-update
  134.3 43.8 %reduce-scatter.2.cloned.1.call-done = f32[128,1024]{1,0:T(8,128)} async-done(((f32[512,1024]{1,0:T(8,128)}), f32[128,1024]{1,0:T(8,128)}) %reduce-scatter.2.cloned.1.call-update) | async-done | bytes 524304 | tf_op jit(solution)/shard_map/reduce_scatter | solution.py:40
  178.1 0.0 copy-done
  178.1 1.3 fusion.7
  179.3 2.1 %fusion.9 = f32[128,1024]{1,0:T(8,128)} fusion(f32[128,1024]{1,0:T(8,128)} %reduce-scatter.2.cloned.1.call-done, f32[128]{0:T(128)S(1)} %fusion.7, f32[128]{0:T(128)S(1)} %get-tuple-element.5, f32[128]{0:T(128)S(1)} %get-tuple-element.6, bf16[128,1024]{1,0:T(8,128)(2,1)S(1)} %copy-done), kind=kLoop, calls=%fused_computation.16 | loop fusion | flops 1048576 | bytes 1312256 | tf_op jit(solution)/shard_map/mul | solution.py:45
  (5 shorter events, 0.0 us)
Async XLA Ops:
  6.5 33.8 %all-gather.7.cloned.1.call-start = ((), (), s32[]{:S(2)}) async-start(), calls=%async_computation.2 | async-start | bytes 1310720 | tf_op jit(solution)/shard_map/all_gather | solution.py:31
  9.4 59.9 %all-gather.5.cloned.1.call-start = ((), (), s32[]{:S(2)}) async-start(), calls=%async_computation.1 | async-start | bytes 2359296 | tf_op jit(solution)/shard_map/all_gather | solution.py:34
  10.2 88.8 %all-gather.11.cloned.1.call-start = ((), (), s32[]{:S(2)}) async-start(), calls=%async_computation.4 | async-start | bytes 1310720 | tf_op jit(solution)/shard_map/all_gather | solution.py:32
  13.2 114.7 %all-gather.9.cloned.1.call-start = ((), (), s32[]{:S(2)}) async-start(), calls=%async_computation.3 | async-start | bytes 2359296 | tf_op jit(solution)/shard_map/all_gather | solution.py:35
  13.8 164.3 %reduce-scatter.2.cloned.1.call-start = ((), (), s32[]{:S(2)}) async-start(), calls=%async_computation.5 | async-start | bytes 2621440 | tf_op jit(solution)/shard_map/reduce_scatter | solution.py:40
  69.4 58.5 %copy-start.1 = (bf16[1024,1024]{1,0:T(8,128)(2,1)S(1)}, bf16[1024,1024]{1,0:T(8,128)(2,1)}, u32[]{:S(2)}) copy-start(bf16[1024,1024]{1,0:T(8,128)(2,1)} %all-gather.5.cloned.1.call-done) | copy-start | bytes 6291460
  134.3 43.8 %copy-start = (bf16[128,1024]{1,0:T(8,128)(2,1)S(1)}, bf16[128,1024]{1,0:T(8,128)(2,1)}, u32[]{:S(2)}) copy-start(bf16[128,1024]{1,0:T(8,128)(2,1)} %param.2) | copy-start | bytes 786436
Sparse Core Ops, SparseCore 0:
  9.6 30.6 all-gather.6
  42.2 27.1 all-gather.4
  71.0 27.9 all-gather.10
  100.7 27.1 all-gather.8
  134.4 43.5 reduce-scatter.1
where the time goes:
time: 188 us
  waiting for transfers between devices  155 us (82%)
  between operations  13.1 us (7%)
  matrix products  11 us (6%)
  other arithmetic  9.13 us (5%)
    reduce_scatter x1, waiting for transfers between devices, local(): pull = lax.psum_scatter(carried, 'gr', scatter_dimension=0, tiled=True)  43.8 us
    all_gather x1, waiting for transfers between devices, local(): piece_s = lax.all_gather(unit_s, 'gc', axis=0, tiled=True)  29.1 us
    all_gather x1, waiting for transfers between devices, local(): piece_t = lax.all_gather(unit_t, 'gc', axis=0, tiled=True)  28.9 us
    all_gather x1, waiting for transfers between devices, local(): lax.all_gather(unit_s, 'gr', axis=0, tiled=True)  26.5 us
    all_gather x1, waiting for transfers between devices, local(): lax.all_gather(unit_t, 'gr', axis=0, tiled=True)  25 us
    dot_general x1, matrix products, local(): lax.dot_general(mismatch, piece_s, (((0,), (0,)), ((), ())), preferred_el...  6.36 us
    dot_general x1, matrix products, mismatch_of(): lax.dot_general(piece_s, other_s, (((1,), (1,)), ((), ())), preferred_ele...  4.6 us
  transfers between devices with their start and end apart: 5, of which 5 were waited for; matrix products, arithmetic and copies ran while one was open for 4% of the time, Pallas kernels for 0%

commit v1 on v0

--- a/solution.py
+++ b/solution.py
@@ -32,7 +32,15 @@
         lax.all_gather(unit_t, "gr", axis=0, tiled=True),
     )
     piece_s = lax.all_gather(unit_s, "gc", axis=0, tiled=True)
-    piece_t = lax.all_gather(unit_t, "gc", axis=0, tiled=True)
+    ways, here = (lax.axis_size("gc"), lax.axis_index("gc"))
+    grown, reach = (unit_t, 1)
+    while reach < ways:
+        theirs = lax.ppermute(grown, "gc", [(d, d ^ reach) for d in range(ways)])
+        mine_first = jnp.concatenate([grown, theirs], axis=0)
+        theirs_first = jnp.concatenate([theirs, grown], axis=0)
+        grown = jnp.where(here & reach == 0, mine_first, theirs_first)
+        reach = 2 * reach
+    piece_t = grown
     mismatch = mismatch_of(piece_s, piece_t, column_s, column_t)
     carried = lax.dot_general(
         mismatch, piece_s, (((0,), (0,)), ((), ())), preferred_element_type=jnp.float32

time: 188 us -> 161 us (0.86)
  waiting for transfers between devices: 155 us -> 123 us
  starting transfers between devices: 0.16 us -> 5.43 us
    all_gather x1 -> x0, waiting for transfers between devices: 28.9 us -> none  [local(): piece_t = lax.all_gather(unit_t, 'gc', axis=0, tiled=True)]
    all_gather x1, waiting for transfers between devices: 26.5 us -> 8.56 us  [local(): lax.all_gather(unit_s, 'gr', axis=0, tiled=True)]
    ppermute x0 -> x3, waiting for transfers between devices: none -> 13.3 us  [local(): theirs = lax.ppermute(grown, 'gc', [(d, d ^ reach) for d in range(ways)])]
    ppermute x0 -> x3, starting transfers between devices: none -> 5.3 us  [local(): theirs = lax.ppermute(grown, 'gc', [(d, d ^ reach) for d in range(ways)])]
    all_gather x1, waiting for transfers between devices: 29.1 us -> 31.8 us  [local(): piece_s = lax.all_gather(unit_s, 'gc', axis=0, tiled=True)]
  transfers between devices with their start and end apart: 5 -> 7, of which waited for: 5 -> 6; matrix products, arithmetic and copies ran while one was open for 4% -> 4% of each run, Pallas kernels for 0% -> 0%
where the time goes in v1:
time: 161 us
  waiting for transfers between devices  123 us (76%)
  between operations  13.2 us (8%)
  matrix products  10.8 us (7%)
  other arithmetic  9 us (6%)
  starting transfers between devices  5.43 us (3%)
    reduce_scatter x1, waiting for transfers between devices, local(): pull = lax.psum_scatter(carried, 'gr', scatter_dimension=0, tiled=True)  43.1 us
    all_gather x1, waiting for transfers between devices, local(): piece_s = lax.all_gather(unit_s, 'gc', axis=0, tiled=True)  31.8 us
    all_gather x1, waiting for transfers between devices, local(): lax.all_gather(unit_t, 'gr', axis=0, tiled=True)  25.1 us
    ppermute x3, waiting for transfers between devices, local(): theirs = lax.ppermute(grown, 'gc', [(d, d ^ reach) for d in range(ways)])  13.3 us
    all_gather x1, waiting for transfers between devices, local(): lax.all_gather(unit_s, 'gr', axis=0, tiled=True)  8.56 us
    dot_general x1, matrix products, local(): lax.dot_general(mismatch, piece_s, (((0,), (0,)), ((), ())), preferred_el...  6.31 us
    ppermute x3, starting transfers between devices, local(): theirs = lax.ppermute(grown, 'gc', [(d, d ^ reach) for d in range(ways)])  5.3 us
    dot_general x1, matrix products, mismatch_of(): lax.dot_general(piece_s, other_s, (((1,), (1,)), ((), ())), preferred_ele...  4.45 us
  transfers between devices with their start and end apart: 7, of which 6 were waited for; matrix products, arithmetic and copies ran while one was open for 4% of the time, Pallas kernels for 0%

profile of v1, /device:TPU:0, one launch (start us, length us, event | category | flops | bytes accessed | tf_op | source)
XLA Modules:
  0.0 161.0 jit_solution(4322727501613220378)
XLA Ops:
  6.5 1.1 fusion.9
  7.6 1.8 %fusion.11 = bf16[128,1024]{1,0:T(8,128)(2,1)} fusion(bf16[128,1024]{1,0:T(8,128)(2,1)} %param.2, f32[128]{0:T(128)S(1)} %get-tuple-element.6), kind=kLoop, calls=%fused_computation.20 | loop fusion | flops 524288 | bytes 524800 | tf_op jit(solution)/shard_map/convert_element_type | solution.py:12
  9.4 0.0 all-gather.4.cloned.1.call-start
  9.5 0.7 all-gather.4.cloned.1.call-update
  10.2 0.0 all-gather.8.cloned.1.call-start
  10.2 1.1 fusion.12
  11.3 1.1 fusion.14
  12.4 0.6 collective-permute-start
  13.0 1.2 collective-permute-done
  14.2 0.1 maximum_select_fusion.7
  14.3 2.9 %collective-permute-start.1 = (bf16[256,1024]{1,0:T(8,128)(2,1)S(1)}, bf16[256,1024]{1,0:T(8,128)(2,1)S(1)}, u32[]{:S(2)}, u32[]{:S(2)}) collective-permute-start(bf16[256,1024]{1,0:T(8,128)(2,1)S(1)} %maximum_select_fusion.7), channel_id=1, source_target_pairs={{0,2},{1,3},{2,0},{3,1},{4,6},{5,7},{6,4},{7,5},{8,10},{9,11},{10,... | collective-permute-start | bytes 1572872 | tf_op jit(solution)/shard_map/ppermute | solution.py:38
  17.2 0.0 all-gather.8.cloned.1.call-update
  17.2 0.0 reduce-scatter.2.cloned.1.call-start
  17.3 12.1 %collective-permute-done.1 = bf16[256,1024]{1,0:T(8,128)(2,1)S(1)} collective-permute-done((bf16[256,1024]{1,0:T(8,128)(2,1)S(1)}, bf16[256,1024]{1,0:T(8,128)(2,1)S(1)}, u32[]{:S(2)}, u32[]{:S(2)}) %collective-permute-start.1) | collective-permute-done | bytes 524320 | tf_op jit(solution)/shard_map/ppermute | solution.py:38
  29.4 0.5 maximum_select_fusion.6
  29.9 1.8 %collective-permute-start.2 = (bf16[512,1024]{1,0:T(8,128)(2,1)S(1)}, bf16[512,1024]{1,0:T(8,128)(2,1)S(1)}, u32[]{:S(2)}, u32[]{:S(2)}) collective-permute-start(bf16[512,1024]{1,0:T(8,128)(2,1)S(1)} %maximum_select_fusion.6), channel_id=1, source_target_pairs={{0,4},{1,5},{2,6},{3,7},{4,0},{5,1},{6,2},{7,3},{8,12},{9,13},{10,... | collective-permute-start | bytes 3145736 | tf_op jit(solution)/shard_map/ppermute | solution.py:38
  31.7 8.6 %all-gather.6.cloned.1.call-done = bf16[512,1024]{1,0:T(8,128)(2,1)} async-done(((bf16[128,1024]{1,0:T(8,128)(2,1)}), bf16[512,1024]{1,0:T(8,128)(2,1)}) %all-gather.6.cloned.1.call-update) | async-done | bytes 1048592 | tf_op jit(solution)/shard_map/all_gather | solution.py:31
  40.3 31.8 %all-gather.4.cloned.1.call-done = bf16[1024,1024]{1,0:T(8,128)(2,1)} async-done(((bf16[128,1024]{1,0:T(8,128)(2,1)}), bf16[1024,1024]{1,0:T(8,128)(2,1)}) %all-gather.4.cloned.1.call-update) | async-done | bytes 2097168 | tf_op jit(solution)/shard_map/all_gather | solution.py:34
  72.1 4.5 %fusion.21 = f32[1024,512]{1,0:T(8,128)} fusion(bf16[1024,1024]{1,0:T(8,128)(2,1)} %all-gather.4.cloned.1.call-done, bf16[512,1024]{1,0:T(8,128)(2,1)} %all-gather.6.cloned.1.call-done), kind=kOutput, calls=%fused_computation.33 | convolution fusion | flops 1073741824 | bytes 5242880 | tf_op jit(solution)/shard_map/dot_general | solution.py:17
  76.5 25.1 %all-gather.8.cloned.1.call-done = bf16[512,1024]{1,0:T(8,128)(2,1)} async-done(((bf16[128,1024]{1,0:T(8,128)(2,1)}), bf16[512,1024]{1,0:T(8,128)(2,1)}) %all-gather.8.cloned.1.call-update) | async-done | bytes 1048592 | tf_op jit(solution)/shard_map/all_gather | solution.py:32
  101.7 6.3 %fusion.7 = f32[512,1024]{1,0:T(8,128)} fusion(bf16[1024,1024]{1,0:T(8,128)(2,1)} %all-gather.4.cloned.1.call-done, f32[1024,512]{1,0:T(8,128)} %fusion.21, bf16[512,1024]{1,0:T(8,128)(2,1)} %all-gather.8.cloned.1.call-done, bf16[512,1024]{1,0:T(8,128)(2,1)S(1)} %collective-permute-done.2, bf16[512,1024]{1,0:T(8,128)(2,1)S(1)} %maximum_select_fusion.6, ...), kind=kOutput, calls=%fused_computation.9 | convolution fusion | flops 2158493696 | bytes 9437185 | tf_op jit(solution)/shard_map/dot_general | solution.py:45
  108.0 43.1 %reduce-scatter.2.cloned.1.call-done = f32[128,1024]{1,0:T(8,128)} async-done(((f32[512,1024]{1,0:T(8,128)}), f32[128,1024]{1,0:T(8,128)}) %reduce-scatter.2.cloned.1.call-update) | async-done | bytes 524304 | tf_op jit(solution)/shard_map/reduce_scatter | solution.py:48
  151.2 1.3 fusion.15
  152.4 2.1 %fusion.17 = f32[128,1024]{1,0:T(8,128)} fusion(f32[128,1024]{1,0:T(8,128)} %reduce-scatter.2.cloned.1.call-done, f32[128]{0:T(128)S(1)} %fusion.15, f32[128]{0:T(128)S(1)} %get-tuple-element.5, f32[128]{0:T(128)S(1)} %get-tuple-element.6, bf16[128,1024]{1,0:T(8,128)(2,1)S(1)} %copy-done), kind=kLoop, calls=%fused_computation.26 | loop fusion | flops 1048576 | bytes 1312256 | tf_op jit(solution)/shard_map/mul | solution.py:53
  (10 shorter events, 0.1 us)
Async XLA Ops:
  6.5 33.8 %all-gather.6.cloned.1.call-start = ((), (), s32[]{:S(2)}) async-start(), calls=%async_computation.2 | async-start | bytes 1310720 | tf_op jit(solution)/shard_map/all_gather | solution.py:31
  9.4 62.7 %all-gather.4.cloned.1.call-start = ((), (), s32[]{:S(2)}) async-start(), calls=%async_computation.1 | async-start | bytes 2359296 | tf_op jit(solution)/shard_map/all_gather | solution.py:34
  10.2 91.5 %all-gather.8.cloned.1.call-start = ((), (), s32[]{:S(2)}) async-start(), calls=%async_computation.3 | async-start | bytes 1310720 | tf_op jit(solution)/shard_map/all_gather | solution.py:32
  12.4 4.8 %copy-start.1 = (bf16[128,1024]{1,0:T(8,128)(2,1)}, bf16[128,1024]{1,0:T(8,128)(2,1)S(1)}, u32[]{:S(2)}) copy-start(bf16[128,1024]{1,0:T(8,128)(2,1)S(1)} %fusion.14) | copy-start | bytes 786436
  12.4 1.7 %collective-permute-start = (bf16[128,1024]{1,0:T(8,128)(2,1)S(1)}, bf16[128,1024]{1,0:T(8,128)(2,1)S(1)}, u32[]{:S(2)}, u32[]{:S(2)}) collective-permute-start(bf16[128,1024]{1,0:T(8,128)(2,1)S(1)} %fusion.14), channel_id=1, source_target_pairs={{0,1},{1,0},{2,3},{3,2},{4,5},{5,4},{6,7},{7,6},{8,9},{9,8},{10,11... | collective-permute-start | bytes 786440 | tf_op jit(solution)/shard_map/ppermute | solution.py:38
  14.3 15.1 %collective-permute-start.1 = (bf16[256,1024]{1,0:T(8,128)(2,1)S(1)}, bf16[256,1024]{1,0:T(8,128)(2,1)S(1)}, u32[]{:S(2)}, u32[]{:S(2)}) collective-permute-start(bf16[256,1024]{1,0:T(8,128)(2,1)S(1)} %maximum_select_fusion.7), channel_id=1, source_target_pairs={{0,2},{1,3},{2,0},{3,1},{4,6},{5,7},{6,4},{7,5},{8,10},{9,11},{10,... | collective-permute-start | bytes 1572872 | tf_op jit(solution)/shard_map/ppermute | solution.py:38
  17.2 133.9 %reduce-scatter.2.cloned.1.call-start = ((), (), s32[]{:S(2)}) async-start(), calls=%async_computation.4 | async-start | bytes 2621440 | tf_op jit(solution)/shard_map/reduce_scatter | solution.py:48
  29.9 71.8 %collective-permute-start.2 = (bf16[512,1024]{1,0:T(8,128)(2,1)S(1)}, bf16[512,1024]{1,0:T(8,128)(2,1)S(1)}, u32[]{:S(2)}, u32[]{:S(2)}) collective-permute-start(bf16[512,1024]{1,0:T(8,128)(2,1)S(1)} %maximum_select_fusion.6), channel_id=1, source_target_pairs={{0,4},{1,5},{2,6},{3,7},{4,0},{5,1},{6,2},{7,3},{8,12},{9,13},{10,... | collective-permute-start | bytes 3145736 | tf_op jit(solution)/shard_map/ppermute | solution.py:38
  108.0 43.2 %copy-start = (bf16[128,1024]{1,0:T(8,128)(2,1)S(1)}, bf16[128,1024]{1,0:T(8,128)(2,1)}, u32[]{:S(2)}) copy-start(bf16[128,1024]{1,0:T(8,128)(2,1)} %param.2) | copy-start | bytes 786436
Sparse Core Ops, SparseCore 0:
  9.6 30.6 all-gather.5
  42.2 29.8 all-gather.3
  73.7 27.9 all-gather.7
  108.1 42.9 reduce-scatter.1
